TPU v7x, 256 devices: a whole 4x4x8 slice. The times are simulated.
256 devices in a mesh: dp: 16 (over z, core), expert: 16 (over y, x).
Axes of the slice: x: 4, y: 4, z: 8, core: 2. Of those that a mesh axis runs over, the one named last changes fastest.
Arguments:
- tokens: bfloat16 [32768, 2048], P(('dp', 'expert')), may hold values from -6 to 6
- expert_ids: int32 [32768, 2], P(('dp', 'expert')), may hold values from 0 to 7, all different within a row; in each aligned block of 128 rows (0 to 127, 128 to 255, ...) at most 40 rows name the same one
- gate_values: bfloat16 [32768, 2], P(('dp', 'expert')), may hold values from 0.19921875 to 0.796875
- w_gate: bfloat16 [16, 2048, 896], P('expert', 'dp'), may hold values from -0.125 to 0.125
- w_up: bfloat16 [16, 2048, 896], P('expert', 'dp'), may hold values from -0.125 to 0.125
- w_down: bfloat16 [16, 896, 2048], P('expert', 'dp'), may hold values from -0.0625 to 0.0625
- cotangent: bfloat16 [32768, 2048], P(('dp', 'expert')), may hold values from -6 to 6
- momentum: bfloat16 [16, 896, 2048], P('expert', 'dp'), may hold values from -4 to 4
- worker_error: bfloat16 [16, 16, 896, 2048], P('dp', 'expert'), may hold values from -2 to 2
- server_error: float32 [16, 896, 2048], P('expert', 'dp'), may hold values from -2 to 2
Outputs:
- outputs: bfloat16 [32768, 2048], P(('dp', 'expert'))
- new_momentum: bfloat16 [16, 896, 2048], P('expert', 'dp')
- new_worker_error: bfloat16 [16, 16, 896, 2048], P('dp', 'expert')
- new_server_error: float32 [16, 896, 2048], P('expert', 'dp')
Inputs may be any that keep to these rules, and one draw needn't show every extreme that they name: `expert_ids`: A token names 2 different experts. Among the 128 tokens of one device at most 40 name the same expert, and some device reaches 40.
All inputs are finite; a program needn't handle non-finite values. Where the computation divides by a largest or mean magnitude, that divisor is 1e-20 or more.
Results may differ from a plain program's by a relative error of at most 0.009.
Values may be sent and summed in bfloat16 or wider, within the bound.
No kernel may reach another device: no remote copies, remote signals or barrier semaphores. Data moves between devices by JAX's collectives and lax.ppermute only.
A program may use at most 128 MiB of HBM per device.

v0:
```python
import jax
import jax.numpy as jnp
import numpy as np
from jax import lax
from jax.sharding import PartitionSpec as P

E = 8
EW = 2
TOP = 2
CAP = 40


def squash(values):
    scale = jnp.mean(jnp.abs(values), axis=-1, keepdims=True) + 1e-06
    return (scale * jnp.tanh(values / scale)).astype(jnp.bfloat16)


def per_device(
    tokens,
    expert_ids,
    gate_values,
    w_gate,
    w_up,
    w_down,
    cotangent,
    momentum,
    worker_error,
    server_error,
):
    n_expert = lax.axis_size("expert")
    n_replica = lax.axis_size("dp")
    tok_count = tokens.shape[0]
    width = tokens.shape[1]
    hidden_units = w_gate.shape[2]
    slots = EW * CAP
    share = n_expert // EW
    flat = expert_ids.reshape(-1)
    onehot = (flat[:, None] == jnp.arange(E, dtype=jnp.int32)[None, :]).astype(jnp.int32)
    ranks = jnp.sum((jnp.cumsum(onehot, axis=0) - onehot) * onehot, axis=1)
    position = jnp.where(flat < EW, flat * CAP + ranks, -1)
    select = (position[None, :] == jnp.arange(slots, dtype=jnp.int32)[:, None]).reshape(
        slots, tok_count, TOP
    )
    dispatch = jnp.any(select, axis=2).astype(jnp.bfloat16)
    combine_w = jnp.sum(jnp.where(select, gate_values.astype(jnp.float32)[None], 0.0), axis=2)
    slot_gates = jnp.sum(combine_w, axis=1).astype(jnp.bfloat16).reshape(EW, CAP)
    peer_owner = np.arange(n_expert) // share
    mix = jnp.asarray((peer_owner[:, None] == np.arange(EW)[None, :]).astype(np.float32)).astype(
        jnp.bfloat16
    )

    def spread(buffer):
        return jnp.take(buffer, jnp.asarray(peer_owner, dtype=jnp.int32), axis=0)

    def slot_rows(source):
        return (
            jnp.dot(dispatch, source, preferred_element_type=jnp.float32)
            .astype(jnp.bfloat16)
            .reshape(EW, CAP, width)
        )

    send_rows = spread(slot_rows(tokens))
    send_gates = spread(slot_gates)
    got_rows, got_gates = (
        lax.all_to_all(send_rows, "expert", split_axis=0, concat_axis=0, tiled=True),
        lax.all_to_all(send_gates, "expert", split_axis=0, concat_axis=0, tiled=True),
    )
    rows = got_rows.reshape(n_expert * CAP, width)
    pieces = (
        lax.all_gather(w_gate, "dp", axis=1, tiled=True),
        lax.all_gather(w_up, "dp", axis=1, tiled=True),
    )
    gate_h = jnp.dot(rows, pieces[0][0], preferred_element_type=jnp.float32)
    up_h = jnp.dot(rows, pieces[1][0], preferred_element_type=jnp.float32)
    hidden = (jax.nn.silu(gate_h) * up_h).astype(jnp.bfloat16)
    down_full, mom_full = (
        lax.all_gather(w_down, "dp", axis=1, tiled=True),
        lax.all_gather(momentum, "dp", axis=1, tiled=True),
    )
    partial_value = jnp.dot(hidden, down_full[0], preferred_element_type=jnp.float32).astype(
        jnp.bfloat16
    )
    returned = lax.all_to_all(
        partial_value.reshape(n_expert, CAP, width),
        "expert",
        split_axis=0,
        concat_axis=0,
        tiled=True,
    )
    expert_sum = jnp.einsum("kcd,ke->ecd", returned, mix, preferred_element_type=jnp.float32)
    outputs = jnp.einsum(
        "pt,pd->td",
        combine_w,
        expert_sum.reshape(slots, width),
        precision=lax.Precision.HIGHEST,
        preferred_element_type=jnp.float32,
    ).astype(jnp.bfloat16)
    got_cot = lax.all_to_all(
        spread(slot_rows(cotangent)), "expert", split_axis=0, concat_axis=0, tiled=True
    )
    dy_rows = got_cot.reshape(n_expert * CAP, width)
    gate_rows = got_gates.reshape(n_expert * CAP).astype(jnp.float32)
    weighted = (hidden.astype(jnp.float32) * gate_rows[:, None]).astype(jnp.bfloat16)
    grad = jnp.einsum("rh,rd->hd", weighted, dy_rows, preferred_element_type=jnp.float32)
    corrected = (
        0.9 * mom_full[0].astype(jnp.float32) + 0.1 * grad + worker_error[0, 0].astype(jnp.float32)
    )
    sent = squash(corrected)
    new_worker = (corrected - sent.astype(jnp.float32)).astype(jnp.bfloat16)[None, None]
    pieces = sent.reshape(n_replica, hidden_units // n_replica, width)
    received = lax.all_to_all(pieces, "dp", split_axis=0, concat_axis=0, tiled=True)
    average = jnp.sum(received.astype(jnp.float32), axis=0) / n_replica
    server_in = average + server_error[0]
    served = squash(server_in)
    new_server = (server_in - served.astype(jnp.float32))[None]
    return (outputs, served[None], new_worker, new_server)


def solution(mesh):
    return jax.shard_map(
        per_device,
        mesh=mesh,
        in_specs=(
            P(("dp", "expert"), None),
            P(("dp", "expert"), None),
            P(("dp", "expert"), None),
            P("expert", "dp", None),
            P("expert", "dp", None),
            P("expert", "dp", None),
            P(("dp", "expert"), None),
            P("expert", "dp", None),
            P("dp", "expert", None, None),
            P("expert", "dp", None),
        ),
        out_specs=(
            P(("dp", "expert"), None),
            P("expert", "dp", None),
            P("dp", "expert", None, None),
            P("expert", "dp", None),
        ),
        check_vma=False,
    )
```

profile of v0, /device:TPU:1, one launch (start us, length us, event | category | flops | bytes accessed | tf_op | source)
XLA Modules:
  0.0 293.4 jit_solution(15084399947835725456)
XLA Ops:
  7.2 0.0 copy-start
  7.2 0.0 all-gather.5.cloned.1.call-start
  7.2 0.7 all-gather.5.cloned.1.call-update
  7.9 0.0 all-gather.7.cloned.1.call-start
  8.0 0.7 all-gather.7.cloned.1.call-update
  8.7 0.0 all-gather.9.cloned.1.call-start
  8.7 0.7 all-gather.9.cloned.1.call-update
  9.4 0.0 all-gather.11.cloned.1.call-start
  9.4 0.5 all-gather.11.cloned.1.call-update
  10.0 0.8 copy.50
  10.8 0.1 eq.43
  10.9 0.1 eq.39
  11.0 0.7 convert_element_type.85
  11.7 0.6 reduce-window.6
  12.3 0.2 slice_reduce_fusion
  12.5 0.1 fusion.19
  12.6 0.1 reduce_sum.57
  12.8 0.1 copy.52
  12.8 0.7 compare_select_fusion
  13.5 0.1 select_reduce_fusion
  13.7 0.1 convert_element_type.94
  13.7 0.7 pad_clamp_fusion
  14.4 0.6 gather_fusion
  15.0 0.6 copy.55
  15.6 7.6 %all-to-all-start.2 = ((bf16[16,1,40]{2,1,0:T(2,128)(2,1)}), bf16[16,1,40]{2,1,0:T(2,128)(2,1)S(1)}, u32[]{:S(2)}, u32[]{:S(2)}) async-start(bf16[16,1,40]{2,1,0:T(2,128)(2,1)} %copy.55), calls=%async_computation.2 | async-start | bytes 16384 | tf_op jit(solution)/shard_map/all_to_all | solution.py:66
  23.2 0.0 copy-done
  23.2 0.2 convolution_convert_fusion.2
  23.5 2.2 gather_fusion.1
  25.7 3.8 %all-to-all-done.2 = bf16[16,1,40]{2,1,0:T(2,128)(2,1)S(1)} async-done(((bf16[16,1,40]{2,1,0:T(2,128)(2,1)}), bf16[16,1,40]{2,1,0:T(2,128)(2,1)S(1)}, u32[]{:S(2)}, u32[]{:S(2)}) %all-to-all-start.2) | async-done | bytes 1312 | tf_op jit(solution)/shard_map/all_to_all | solution.py:66
  29.5 3.8 %all-to-all-start = ((bf16[16,40,2048]{2,1,0:T(8,128)(2,1)}), bf16[16,40,2048]{2,1,0:T(8,128)(2,1)S(1)}, u32[]{:S(2)}, u32[]{:S(2)}) async-start(bf16[16,40,2048]{2,1,0:T(8,128)(2,1)} %gather_fusion.1), calls=%async_computation | async-start | bytes 5242880 | tf_op jit(solution)/shard_map/all_to_all | solution.py:65
  33.3 1.3 convolution_convert_fusion.1
  34.6 2.2 gather_fusion.2
  36.8 31.5 %all-to-all-done = bf16[16,40,2048]{2,1,0:T(8,128)(2,1)S(1)} async-done(((bf16[16,40,2048]{2,1,0:T(8,128)(2,1)}), bf16[16,40,2048]{2,1,0:T(8,128)(2,1)S(1)}, u32[]{:S(2)}, u32[]{:S(2)}) %all-to-all-start) | async-done | bytes 2621472 | tf_op jit(solution)/shard_map/all_to_all | solution.py:65
  68.3 0.0 copy-start.2
  68.3 1.5 copy-done.2
  69.8 5.5 %all-to-all-start.3 = ((bf16[16,40,2048]{2,1,0:T(8,128)(2,1)}), bf16[16,40,2048]{2,1,0:T(8,128)(2,1)S(1)}, u32[]{:S(2)}, u32[]{:S(2)}) async-start(bf16[16,40,2048]{2,1,0:T(8,128)(2,1)} %gather_fusion.2), calls=%async_computation.3 | async-start | bytes 5242880 | tf_op jit(solution)/shard_map/all_to_all | solution.py:98
  75.3 0.0 all-gather.5.cloned.1.call-done
  75.3 7.2 %fusion.5 = f32[640,896]{1,0:T(8,128)} fusion(bf16[640,2048]{1,0:T(8,128)(2,1)} %bitcast.68, bf16[1,2048,896]{2,1,0:T(8,128)(2,1)} %all-gather.5.cloned.1.call-done), kind=kOutput, calls=%fused_computation.14 | convolution fusion | flops 2348810240 | bytes 8585216 | tf_op jit(solution)/shard_map/dot_general | solution.py:73
  82.5 14.8 %all-gather.7.cloned.1.call-done = bf16[1,2048,896]{2,1,0:T(8,128)(2,1)} async-done(((bf16[1,128,896]{2,1,0:T(8,128)(2,1)}), bf16[1,2048,896]{2,1,0:T(8,128)(2,1)}) %all-gather.7.cloned.1.call-update) | async-done | bytes 3670032 | tf_op jit(solution)/shard_map/all_gather | solution.py:71
  97.3 7.5 %multiply_convert_fusion.2 = bf16[640,896]{1,0:T(8,128)(2,1)} fusion(f32[640,896]{1,0:T(8,128)} %fusion.5, bf16[640,2048]{1,0:T(8,128)(2,1)} %bitcast.69, bf16[1,2048,896]{2,1,0:T(8,128)(2,1)} %all-gather.7.cloned.1.call-done), kind=kOutput, calls=%fused_computation.23 | convolution fusion | flops 2352250880 | bytes 9732096 | tf_op jit(solution)/shard_map/dot_general | solution.py:74
  104.8 35.1 %all-gather.9.cloned.1.call-done = bf16[1,896,2048]{2,1,0:T(8,128)(2,1)} async-done(((bf16[1,56,2048]{2,1,0:T(8,128)(2,1)}), bf16[1,896,2048]{2,1,0:T(8,128)(2,1)}) %all-gather.9.cloned.1.call-update) | async-done | bytes 3670032 | tf_op jit(solution)/shard_map/all_gather | solution.py:77
  139.8 6.8 %fusion.7 = bf16[640,2048]{1,0:T(8,128)(2,1)} fusion(bf16[640,896]{1,0:T(8,128)(2,1)} %multiply_convert_fusion.2, bf16[1,896,2048]{2,1,0:T(8,128)(2,1)} %all-gather.9.cloned.1.call-done), kind=kOutput, calls=%fused_computation.16 | convolution fusion | flops 2350120960 | bytes 7438336 | tf_op jit(solution)/shard_map/dot_general | solution.py:80
  146.6 0.0 all-to-all-done.3
  146.6 0.0 copy-start.1
  146.6 1.5 copy-done.1
  148.1 6.5 %all-to-all-start.1 = ((bf16[16,40,2048]{2,1,0:T(8,128)(2,1)}), bf16[16,40,2048]{2,1,0:T(8,128)(2,1)S(1)}, u32[]{:S(2)}, u32[]{:S(2)}) async-start(bf16[16,40,2048]{2,1,0:T(8,128)(2,1)} %bitcast.67), calls=%async_computation.1 | async-start | bytes 5242880 | tf_op jit(solution)/shard_map/all_to_all | solution.py:83
  154.7 0.1 reshape.180
  154.8 26.9 %all-gather.11.cloned.1.call-done = bf16[1,896,2048]{2,1,0:T(8,128)(2,1)} async-done(((bf16[1,56,2048]{2,1,0:T(8,128)(2,1)}), bf16[1,896,2048]{2,1,0:T(8,128)(2,1)}) %all-gather.11.cloned.1.call-update) | async-done | bytes 3670032 | tf_op jit(solution)/shard_map/all_gather | solution.py:78
  181.7 8.9 %abs_reduce_fusion = (f32[896]{0:T(1024)S(1)}, f32[896,2048]{1,0:T(8,128)S(1)}) fusion(bf16[1,1,896,2048]{3,2,1,0:T(8,128)(2,1)} %param.24, bf16[640,2048]{1,0:T(8,128)(2,1)} %bitcast.66, bf16[640,896]{1,0:T(8,128)(2,1)} %multiply_convert_fusion.2, f32[640]{0:T(1024)S(1)} %reshape.180, bf16[1,896,2048]{2,1,0:T(8,128)(2,1)} %all-gather.11.cloned.1.call-done), kind=kOutput, calls=%fused_computation.8 | convolution fusion | flops 2365209600 | bytes 18454528 | tf_op jit(solution)/shard_map/rh,rd->hd/dot_general | solution.py:104
  190.6 3.9 %fusion = (bf16[1,1,896,2048]{3,2,1,0:T(8,128)(2,1)}, bf16[896,2048]{1,0:T(8,128)(2,1)}) fusion(f32[896,2048]{1,0:T(8,128)S(1)} %get-tuple-element.12, f32[896]{0:T(1024)S(1)} %multiply_add_fusion), kind=kLoop, calls=%fused_computation.9 | loop fusion | flops 11010048 | bytes 14683648 | tf_op jit(solution)/shard_map/broadcast_in_dim | solution.py:109
  194.5 0.3 all-to-all-done.1
  194.7 0.0 copy-start.4
  194.7 5.8 %all-to-all-start.4 = ((bf16[16,56,2048]{2,1,0:T(8,128)(2,1)}), bf16[16,56,2048]{2,1,0:T(8,128)(2,1)}, u32[]{:S(2)}, u32[]{:S(2)}) async-start(bf16[16,56,2048]{2,1,0:T(8,128)(2,1)} %bitcast.65), calls=%async_computation.4 | async-start | bytes 7340032 | tf_op jit(solution)/shard_map/all_to_all | solution.py:111
  200.6 0.0 copy-done.4
  200.6 3.0 %fusion.10 = f32[2,40,2048]{2,0,1:T(2,128)S(1)} fusion(bf16[16,2,1]{0,1,2:T(2,128)(2,1)S(1)} %copy-done.4, bf16[16,40,2048]{2,1,0:T(8,128)(2,1)S(1)} %all-to-all-done.1), kind=kOutput, calls=%fused_computation.17 | convolution fusion | flops 5242880 | bytes 3276864 | tf_op jit(solution)/shard_map/kcd,ke->ecd/dot_general | solution.py:90
  203.5 0.4 copy.54
  203.9 0.0 copy-start.3
  203.9 1.8 convolution_convert_fusion
  205.8 77.2 %all-to-all-done.4 = bf16[16,56,2048]{2,1,0:T(8,128)(2,1)} async-done(((bf16[16,56,2048]{2,1,0:T(8,128)(2,1)}), bf16[16,56,2048]{2,1,0:T(8,128)(2,1)}, u32[]{:S(2)}, u32[]{:S(2)}) %all-to-all-start.4) | async-done | bytes 3670048 | tf_op jit(solution)/shard_map/all_to_all | solution.py:111
  282.9 2.8 convert_reduce_fusion
  285.7 0.0 copy-done.3
  285.7 0.2 fusion.16
  285.9 1.0 convert_subtract_fusion
  (7 shorter events, 0.1 us)
Async XLA Ops:
  7.2 16.0 %copy-start = (bf16[128,2048]{1,0:T(8,128)(2,1)S(1)}, bf16[128,2048]{1,0:T(8,128)(2,1)}, u32[]{:S(2)}) copy-start(bf16[128,2048]{1,0:T(8,128)(2,1)} %param.16) | copy-start | bytes 1572868
  7.2 68.2 %all-gather.5.cloned.1.call-start = ((), (), s32[]{:S(2)}) async-start(), calls=%async_computation.5 | async-start | bytes 3899392 | tf_op jit(solution)/shard_map/all_gather | solution.py:70
  7.9 89.4 %all-gather.7.cloned.1.call-start = ((), (), s32[]{:S(2)}) async-start(), calls=%async_computation.6 | async-start | bytes 3899392 | tf_op jit(solution)/shard_map/all_gather | solution.py:71
  8.7 131.2 %all-gather.9.cloned.1.call-start = ((), (), s32[]{:S(2)}) async-start(), calls=%async_computation.7 | async-start | bytes 3899392 | tf_op jit(solution)/shard_map/all_gather | solution.py:77
  9.4 172.3 %all-gather.11.cloned.1.call-start = ((), (), s32[]{:S(2)}) async-start(), calls=%async_computation.8 | async-start | bytes 3899392 | tf_op jit(solution)/shard_map/all_gather | solution.py:78
  15.6 13.9 %all-to-all-start.2 = ((bf16[16,1,40]{2,1,0:T(2,128)(2,1)}), bf16[16,1,40]{2,1,0:T(2,128)(2,1)S(1)}, u32[]{:S(2)}, u32[]{:S(2)}) async-start(bf16[16,1,40]{2,1,0:T(2,128)(2,1)} %copy.55), calls=%async_computation.2 | async-start | bytes 16384 | tf_op jit(solution)/shard_map/all_to_all | solution.py:66
  29.5 38.8 %all-to-all-start = ((bf16[16,40,2048]{2,1,0:T(8,128)(2,1)}), bf16[16,40,2048]{2,1,0:T(8,128)(2,1)S(1)}, u32[]{:S(2)}, u32[]{:S(2)}) async-start(bf16[16,40,2048]{2,1,0:T(8,128)(2,1)} %gather_fusion.1), calls=%async_computation | async-start | bytes 5242880 | tf_op jit(solution)/shard_map/all_to_all | solution.py:65
  68.3 1.5 copy-start.2
  69.8 76.9 %all-to-all-start.3 = ((bf16[16,40,2048]{2,1,0:T(8,128)(2,1)}), bf16[16,40,2048]{2,1,0:T(8,128)(2,1)S(1)}, u32[]{:S(2)}, u32[]{:S(2)}) async-start(bf16[16,40,2048]{2,1,0:T(8,128)(2,1)} %gather_fusion.2), calls=%async_computation.3 | async-start | bytes 5242880 | tf_op jit(solution)/shard_map/all_to_all | solution.py:98
  146.6 1.5 copy-start.1
  148.1 46.6 %all-to-all-start.1 = ((bf16[16,40,2048]{2,1,0:T(8,128)(2,1)}), bf16[16,40,2048]{2,1,0:T(8,128)(2,1)S(1)}, u32[]{:S(2)}, u32[]{:S(2)}) async-start(bf16[16,40,2048]{2,1,0:T(8,128)(2,1)} %bitcast.67), calls=%async_computation.1 | async-start | bytes 5242880 | tf_op jit(solution)/shard_map/all_to_all | solution.py:83
  194.7 5.8 %copy-start.4 = (bf16[16,2,1]{0,1,2:T(2,128)(2,1)S(1)}, bf16[16,2,1]{0,1,2:T(2,128)(2,1)}, u32[]{:S(2)}) copy-start(bf16[16,2,1]{0,1,2:T(2,128)(2,1)} %constant.104) | copy-start | bytes 196
  194.7 88.2 %all-to-all-start.4 = ((bf16[16,56,2048]{2,1,0:T(8,128)(2,1)}), bf16[16,56,2048]{2,1,0:T(8,128)(2,1)}, u32[]{:S(2)}, u32[]{:S(2)}) async-start(bf16[16,56,2048]{2,1,0:T(8,128)(2,1)} %bitcast.65), calls=%async_computation.4 | async-start | bytes 7340032 | tf_op jit(solution)/shard_map/all_to_all | solution.py:111
  203.9 81.8 %copy-start.3 = (f32[1,56,2048]{2,1,0:T(8,128)S(1)}, f32[1,56,2048]{2,1,0:T(8,128)}, u32[]{:S(2)}) copy-start(f32[1,56,2048]{2,1,0:T(8,128)} %param.25) | copy-start | bytes 1376260
Sparse Core Ops, SparseCore 0:
  9.8 45.3 all-gather.4
  57.1 40.1 all-gather.6
  99.1 40.6 all-gather.8
  141.5 40.1 all-gather.10
where the time goes:
time: 294 us; the launch traced here: 293 us
  waiting for transfers between devices  192 us (65%)
  matrix products  36.6 us (12%)
  starting transfers between devices  29.4 us (10%)
  between operations  13.9 us (5%)
  other arithmetic  10.7 us (4%)
  local copies, waits for them, and re-layouts  10.6 us (4%)
    all_to_all x1, waiting for transfers between devices, per_device(): lax.all_to_all(pieces, 'dp', split_axis=0, concat_axis=0, tiled=True)  77.2 us
    all_gather x1, waiting for transfers between devices, per_device(): lax.all_gather(w_down, 'dp', axis=1, tiled=True)  35.1 us
    all_to_all x1, waiting for transfers between devices, per_device(): lax.all_to_all(send_rows, 'expert', split_axis=0, concat_axis=0, tiled=True)  31.5 us
    all_gather x1, waiting for transfers between devices, per_device(): lax.all_gather(momentum, 'dp', axis=1, tiled=True)  26.9 us
    all_gather x1, waiting for transfers between devices, per_device(): lax.all_gather(w_up, 'dp', axis=1, tiled=True)  14.8 us
    dot_general x1, matrix products, per_device(): jnp.einsum('rh,rd->hd', weighted, dy_rows, preferred_element_type=jnp.flo...  8.87 us
    all_to_all x1, starting transfers between devices, per_device(): lax.all_to_all(send_gates, 'expert', split_axis=0, concat_axis=0, tiled=T...  7.58 us
    dot_general x1, matrix products, per_device(): up_h = jnp.dot(rows, pieces[1][0], preferred_element_type=jnp.float32)  7.46 us
  transfers between devices with their start and end apart: 9, of which 7 were waited for; matrix products, arithmetic and copies ran while one was open for 17% of the time, Pallas kernels for 0%

commit v1 on v0

--- a/solution.py
+++ b/solution.py
@@ -8,6 +8,11 @@
 EW = 2
 TOP = 2
 CAP = 40
+
+
+def exchange_gather(x, axis, along):
+    repeated = jnp.stack([x] * lax.axis_size(axis))
+    return jnp.concatenate(lax.all_to_all(repeated, axis, 0, 0), axis=along)
 
 
 def squash(values):
@@ -66,10 +71,7 @@
         lax.all_to_all(send_gates, "expert", split_axis=0, concat_axis=0, tiled=True),
     )
     rows = got_rows.reshape(n_expert * CAP, width)
-    pieces = (
-        lax.all_gather(w_gate, "dp", axis=1, tiled=True),
-        lax.all_gather(w_up, "dp", axis=1, tiled=True),
-    )
+    pieces = (lax.all_gather(w_gate, "dp", axis=1, tiled=True), exchange_gather(w_up, "dp", 1))
     gate_h = jnp.dot(rows, pieces[0][0], preferred_element_type=jnp.float32)
     up_h = jnp.dot(rows, pieces[1][0], preferred_element_type=jnp.float32)
     hidden = (jax.nn.silu(gate_h) * up_h).astype(jnp.bfloat16)

time: 294 us -> 365 us (1.24)
  blocking collectives: 0 us -> 36.6 us
  waiting for transfers between devices: 192 us -> 224 us
  starting transfers between devices: 29.4 us -> 36.1 us
  matrix products: 36.6 us -> 32.9 us
    all_to_all x1, waiting for transfers between devices: 31.5 us -> 94 us  [exchange_gather(): return jnp.concatenate(lax.all_to_all(repeated, axis, 0, 0), axis=along)]
    all_to_all x0 -> x1, blocking collectives: none -> 36.6 us  [per_device(): lax.all_to_all(send_rows, 'expert', split_axis=0, concat_axis=0, tiled=True)]
    all_gather x1, waiting for transfers between devices: 35.1 us -> 0.01 us  [per_device(): lax.all_gather(w_down, 'dp', axis=1, tiled=True)]
    all_gather x1, waiting for transfers between devices: 26.9 us -> 0.02 us  [per_device(): lax.all_gather(momentum, 'dp', axis=1, tiled=True)]
    all_to_all x1, waiting for transfers between devices: 0.27 us -> 23.7 us  [per_device(): lax.all_to_all(partial_value.reshape(n_expert, CAP, width), 'expert', spl...]
    all_to_all x1, waiting for transfers between devices: 0.01 us -> 21.5 us  [per_device(): lax.all_to_all(spread(slot_rows(cotangent)), 'expert', split_axis=0, conc...]
    all_gather x1 -> x0, waiting for transfers between devices: 14.8 us -> none  [per_device(): lax.all_gather(w_up, 'dp', axis=1, tiled=True)]
    all_to_all x1, starting transfers between devices: 3.76 us -> 11.2 us  [exchange_gather(): return jnp.concatenate(lax.all_to_all(repeated, axis, 0, 0), axis=along)]
  transfers between devices with their start and end apart: 9 -> 8, of which waited for: 7 -> 5; matrix products, arithmetic and copies ran while one was open for 17% -> 13% of each run, Pallas kernels for 0% -> 0%
where the time goes in v1:
time: 365 us; the launch traced here: 364 us
  waiting for transfers between devices  224 us (61%)
  blocking collectives  36.6 us (10%)
  starting transfers between devices  36.1 us (10%)
  matrix products  32.9 us (9%)
  between operations  14 us (4%)
  other arithmetic  10.7 us (3%)
  local copies, waits for them, and re-layouts  9.99 us (3%)
    all_to_all x1, waiting for transfers between devices, exchange_gather(): return jnp.concatenate(lax.all_to_all(repeated, axis, 0, 0), axis=along)  94 us
    all_to_all x1, waiting for transfers between devices, per_device(): lax.all_to_all(pieces, 'dp', split_axis=0, concat_axis=0, tiled=True)  77.2 us
    all_to_all x1, blocking collectives, per_device(): lax.all_to_all(send_rows, 'expert', split_axis=0, concat_axis=0, tiled=True)  36.6 us
    all_to_all x1, waiting for transfers between devices, per_device(): lax.all_to_all(partial_value.reshape(n_expert, CAP, width), 'expert', spl...  23.7 us
    all_to_all x1, waiting for transfers between devices, per_device(): lax.all_to_all(spread(slot_rows(cotangent)), 'expert', split_axis=0, conc...  21.5 us
    all_to_all x1, starting transfers between devices, exchange_gather(): return jnp.concatenate(lax.all_to_all(repeated, axis, 0, 0), axis=along)  11.2 us
    dot_general x1, matrix products, per_device(): jnp.einsum('rh,rd->hd', weighted, dy_rows, preferred_element_type=jnp.flo...  8.88 us
    all_to_all x1, starting transfers between devices, per_device(): lax.all_to_all(pieces, 'dp', split_axis=0, concat_axis=0, tiled=True)  8.87 us
  transfers between devices with their start and end apart: 8, of which 5 were waited for; matrix products, arithmetic and copies ran while one was open for 13% of the time, Pallas kernels for 0%

profile of v1, /device:TPU:1, one launch (start us, length us, event | category | flops | bytes accessed | tf_op | source)
XLA Modules:
  0.0 364.0 jit_solution(7757475522727023207)
XLA Ops:
  7.2 0.0 copy-start
  7.2 0.0 all-gather.4.cloned.1.call-start
  7.2 0.7 all-gather.4.cloned.1.call-update
  7.9 0.0 all-gather.6.cloned.1.call-start
  8.0 0.7 all-gather.6.cloned.1.call-update
  8.7 0.8 copy.50
  9.5 0.1 eq.43
  9.6 0.1 eq.39
  9.7 0.7 convert_element_type.85
  10.4 0.6 reduce-window.6
  11.0 0.2 slice_reduce_fusion
  11.2 0.1 fusion.15
  11.3 0.1 reduce_sum.57
  11.5 0.1 copy.52
  11.5 0.7 compare_select_fusion
  12.2 0.1 select_reduce_fusion
  12.3 0.1 convert_element_type.94
  12.4 0.7 pad_clamp_fusion
  13.1 0.6 gather_fusion
  13.7 0.6 copy.55
  14.3 7.6 %all-to-all-start.3 = ((bf16[16,1,40]{2,1,0:T(2,128)(2,1)}), bf16[16,1,40]{2,1,0:T(2,128)(2,1)S(1)}, u32[]{:S(2)}, u32[]{:S(2)}) async-start(bf16[16,1,40]{2,1,0:T(2,128)(2,1)} %copy.55), calls=%async_computation.3 | async-start | bytes 16384 | tf_op jit(solution)/shard_map/all_to_all | solution.py:71
  21.9 0.0 copy-done
  21.9 0.2 convolution_convert_fusion.2
  22.2 0.7 gather_fusion.1
  22.9 0.0 copy-start.5
  22.9 5.3 %all-to-all-done.3 = bf16[16,1,40]{2,1,0:T(2,128)(2,1)S(1)} async-done(((bf16[16,1,40]{2,1,0:T(2,128)(2,1)}), bf16[16,1,40]{2,1,0:T(2,128)(2,1)S(1)}, u32[]{:S(2)}, u32[]{:S(2)}) %all-to-all-start.3) | async-done | bytes 1312 | tf_op jit(solution)/shard_map/all_to_all | solution.py:71
  28.2 36.6 %all_to_all.31 = bf16[16,40,2048]{2,1,0:T(8,128)(2,1)} all-to-all(bf16[16,40,2048]{2,1,0:T(8,128)(2,1)S(1)} %gather_fusion.1), channel_id=1, replica_groups=mesh['dp'=16,'expert'=16] {'expert'}, dimensions={0} | all-to-all | bytes 5242880 | tf_op jit(solution)/shard_map/all_to_all | solution.py:70
  64.8 0.0 copy-done.5
  64.8 2.3 stack.2
  67.2 0.0 copy-start.4
  67.2 11.2 %all-to-all-start.1 = ((bf16[16,1,128,896]{3,2,1,0:T(8,128)(2,1)}), bf16[16,1,128,896]{3,2,1,0:T(8,128)(2,1)}, u32[]{:S(2)}, u32[]{:S(2)}) async-start(bf16[16,1,128,896]{3,2,1,0:T(8,128)(2,1)} %stack.2), calls=%async_computation.1 | async-start | bytes 7340032 | tf_op jit(solution)/shard_map/all_to_all | solution.py:15
  78.4 0.0 all-gather.8.cloned.1.call-start
  78.5 0.7 all-gather.8.cloned.1.call-update
  79.2 0.0 copy-done.4
  79.2 0.2 convolution_convert_fusion.1
  79.4 2.2 gather_fusion.2
  81.6 94.0 %all-to-all-done.1 = bf16[16,1,128,896]{3,2,1,0:T(8,128)(2,1)} async-done(((bf16[16,1,128,896]{3,2,1,0:T(8,128)(2,1)}), bf16[16,1,128,896]{3,2,1,0:T(8,128)(2,1)}, u32[]{:S(2)}, u32[]{:S(2)}) %all-to-all-start.1) | async-done | bytes 3670048 | tf_op jit(solution)/shard_map/all_to_all | solution.py:15
  175.6 4.2 %all-to-all-start.4 = ((bf16[16,40,2048]{2,1,0:T(8,128)(2,1)}), bf16[16,40,2048]{2,1,0:T(8,128)(2,1)S(1)}, u32[]{:S(2)}, u32[]{:S(2)}) async-start(bf16[16,40,2048]{2,1,0:T(8,128)(2,1)} %gather_fusion.2), calls=%async_computation.4 | async-start | bytes 5242880 | tf_op jit(solution)/shard_map/all_to_all | solution.py:100
  179.8 0.0 all-gather.4.cloned.1.call-done
  179.8 0.0 copy-start.2
  179.8 5.9 %fusion.3 = f32[640,896]{1,0:T(8,128)S(1)} fusion(bf16[640,2048]{1,0:T(8,128)(2,1)} %bitcast.65, bf16[1,2048,896]{2,1,0:T(8,128)(2,1)} %all-gather.4.cloned.1.call-done), kind=kOutput, calls=%fused_computation.12 | convolution fusion | flops 2348810240 | bytes 8585216 | tf_op jit(solution)/shard_map/dot_general | solution.py:75
  185.7 0.0 copy-done.2
  185.7 6.1 %multiply_convert_fusion.2 = bf16[640,896]{1,0:T(8,128)(2,1)} fusion(f32[640,896]{1,0:T(8,128)S(1)} %fusion.3, bf16[640,2048]{1,0:T(8,128)(2,1)S(1)} %bitcast.66, bf16[2048,896]{1,0:T(8,128)(2,1)} %bitcast.7), kind=kOutput, calls=%fused_computation.21 | convolution fusion | flops 2352250880 | bytes 9732096 | tf_op jit(solution)/shard_map/dot_general | solution.py:76
  191.8 0.0 all-gather.6.cloned.1.call-done
  191.8 6.8 %fusion.5 = bf16[640,2048]{1,0:T(8,128)(2,1)} fusion(bf16[640,896]{1,0:T(8,128)(2,1)} %multiply_convert_fusion.2, bf16[1,896,2048]{2,1,0:T(8,128)(2,1)} %all-gather.6.cloned.1.call-done), kind=kOutput, calls=%fused_computation.14 | convolution fusion | flops 2350120960 | bytes 7438336 | tf_op jit(solution)/shard_map/dot_general | solution.py:82
  198.6 21.5 %all-to-all-done.4 = bf16[16,40,2048]{2,1,0:T(8,128)(2,1)S(1)} async-done(((bf16[16,40,2048]{2,1,0:T(8,128)(2,1)}), bf16[16,40,2048]{2,1,0:T(8,128)(2,1)S(1)}, u32[]{:S(2)}, u32[]{:S(2)}) %all-to-all-start.4) | async-done | bytes 2621472 | tf_op jit(solution)/shard_map/all_to_all | solution.py:100
  220.1 1.5 copy-done.1
  221.6 4.1 %all-to-all-start.2 = ((bf16[16,40,2048]{2,1,0:T(8,128)(2,1)}), bf16[16,40,2048]{2,1,0:T(8,128)(2,1)S(1)}, u32[]{:S(2)}, u32[]{:S(2)}) async-start(bf16[16,40,2048]{2,1,0:T(8,128)(2,1)} %bitcast.67), calls=%async_computation.2 | async-start | bytes 5242880 | tf_op jit(solution)/shard_map/all_to_all | solution.py:85
  225.7 0.1 reshape.183
  225.8 0.0 all-gather.8.cloned.1.call-done
  225.8 8.9 %abs_reduce_fusion = (f32[896]{0:T(1024)S(1)}, f32[896,2048]{1,0:T(8,128)S(1)}) fusion(bf16[1,1,896,2048]{3,2,1,0:T(8,128)(2,1)} %param.24, bf16[640,2048]{1,0:T(8,128)(2,1)} %bitcast.64, bf16[640,896]{1,0:T(8,128)(2,1)} %multiply_convert_fusion.2, f32[640]{0:T(1024)S(1)} %reshape.183, bf16[1,896,2048]{2,1,0:T(8,128)(2,1)} %all-gather.8.cloned.1.call-done), kind=kOutput, calls=%fused_computation.8 | convolution fusion | flops 2365209600 | bytes 18454528 | tf_op jit(solution)/shard_map/rh,rd->hd/dot_general | solution.py:106
  234.7 3.9 %fusion = (bf16[1,1,896,2048]{3,2,1,0:T(8,128)(2,1)}, bf16[896,2048]{1,0:T(8,128)(2,1)}) fusion(f32[896,2048]{1,0:T(8,128)S(1)} %get-tuple-element.12, f32[896]{0:T(1024)S(1)} %multiply_add_fusion), kind=kLoop, calls=%fused_computation.9 | loop fusion | flops 11010048 | bytes 14683648 | tf_op jit(solution)/shard_map/broadcast_in_dim | solution.py:111
  238.6 23.7 %all-to-all-done.2 = bf16[16,40,2048]{2,1,0:T(8,128)(2,1)S(1)} async-done(((bf16[16,40,2048]{2,1,0:T(8,128)(2,1)}), bf16[16,40,2048]{2,1,0:T(8,128)(2,1)S(1)}, u32[]{:S(2)}, u32[]{:S(2)}) %all-to-all-start.2) | async-done | bytes 2621472 | tf_op jit(solution)/shard_map/all_to_all | solution.py:85
  262.3 8.9 %all-to-all-start.5 = ((bf16[16,56,2048]{2,1,0:T(8,128)(2,1)}), bf16[16,56,2048]{2,1,0:T(8,128)(2,1)}, u32[]{:S(2)}, u32[]{:S(2)}) async-start(bf16[16,56,2048]{2,1,0:T(8,128)(2,1)} %bitcast.63), calls=%async_computation.5 | async-start | bytes 7340032 | tf_op jit(solution)/shard_map/all_to_all | solution.py:113
  271.1 0.0 copy-done.6
  271.1 3.0 fusion.8
  274.1 0.4 copy.54
  274.5 0.0 copy-start.3
  274.5 1.8 convolution_convert_fusion
  276.3 77.2 %all-to-all-done.5 = bf16[16,56,2048]{2,1,0:T(8,128)(2,1)} async-done(((bf16[16,56,2048]{2,1,0:T(8,128)(2,1)}), bf16[16,56,2048]{2,1,0:T(8,128)(2,1)}, u32[]{:S(2)}, u32[]{:S(2)}) %all-to-all-start.5) | async-done | bytes 3670048 | tf_op jit(solution)/shard_map/all_to_all | solution.py:113
  353.5 2.8 convert_reduce_fusion
  356.3 0.0 copy-done.3
  356.3 0.2 fusion.12
  356.5 1.0 convert_subtract_fusion
  (9 shorter events, 0.1 us)
Async XLA Ops:
  7.2 14.7 %copy-start = (bf16[128,2048]{1,0:T(8,128)(2,1)S(1)}, bf16[128,2048]{1,0:T(8,128)(2,1)}, u32[]{:S(2)}) copy-start(bf16[128,2048]{1,0:T(8,128)(2,1)} %param.16) | copy-start | bytes 1572868
  7.2 172.6 %all-gather.4.cloned.1.call-start = ((), (), s32[]{:S(2)}) async-start(), calls=%async_computation.6 | async-start | bytes 3899392 | tf_op jit(solution)/shard_map/all_gather | solution.py:74
  7.9 183.9 %all-gather.6.cloned.1.call-start = ((), (), s32[]{:S(2)}) async-start(), calls=%async_computation.7 | async-start | bytes 3899392 | tf_op jit(solution)/shard_map/all_gather | solution.py:79
  14.3 13.9 %all-to-all-start.3 = ((bf16[16,1,40]{2,1,0:T(2,128)(2,1)}), bf16[16,1,40]{2,1,0:T(2,128)(2,1)S(1)}, u32[]{:S(2)}, u32[]{:S(2)}) async-start(bf16[16,1,40]{2,1,0:T(2,128)(2,1)} %copy.55), calls=%async_computation.3 | async-start | bytes 16384 | tf_op jit(solution)/shard_map/all_to_all | solution.py:71
  22.9 42.0 %copy-start.5 = (bf16[1,128,896]{2,1,0:T(8,128)(2,1)S(1)}, bf16[1,128,896]{2,1,0:T(8,128)(2,1)}, u32[]{:S(2)}) copy-start(bf16[1,128,896]{2,1,0:T(8,128)(2,1)} %param.20) | copy-start | bytes 688132
  67.2 12.0 %copy-start.4 = (bf16[128,2048]{1,0:T(8,128)(2,1)S(1)}, bf16[128,2048]{1,0:T(8,128)(2,1)}, u32[]{:S(2)}) copy-start(bf16[128,2048]{1,0:T(8,128)(2,1)} %param.22) | copy-start | bytes 1572868
  67.2 108.4 %all-to-all-start.1 = ((bf16[16,1,128,896]{3,2,1,0:T(8,128)(2,1)}), bf16[16,1,128,896]{3,2,1,0:T(8,128)(2,1)}, u32[]{:S(2)}, u32[]{:S(2)}) async-start(bf16[16,1,128,896]{3,2,1,0:T(8,128)(2,1)} %stack.2), calls=%async_computation.1 | async-start | bytes 7340032 | tf_op jit(solution)/shard_map/all_to_all | solution.py:15
  78.4 147.4 %all-gather.8.cloned.1.call-start = ((), (), s32[]{:S(2)}) async-start(), calls=%async_computation.8 | async-start | bytes 3899392 | tf_op jit(solution)/shard_map/all_gather | solution.py:80
  175.6 44.5 %all-to-all-start.4 = ((bf16[16,40,2048]{2,1,0:T(8,128)(2,1)}), bf16[16,40,2048]{2,1,0:T(8,128)(2,1)S(1)}, u32[]{:S(2)}, u32[]{:S(2)}) async-start(bf16[16,40,2048]{2,1,0:T(8,128)(2,1)} %gather_fusion.2), calls=%async_computation.4 | async-start | bytes 5242880 | tf_op jit(solution)/shard_map/all_to_all | solution.py:100
  179.8 5.9 %copy-start.2 = (bf16[16,40,2048]{2,1,0:T(8,128)(2,1)S(1)}, bf16[16,40,2048]{2,1,0:T(8,128)(2,1)}, u32[]{:S(2)}) copy-start(bf16[16,40,2048]{2,1,0:T(8,128)(2,1)} %all_to_all.31) | copy-start | bytes 7864324
  220.1 1.5 copy-start.1
  221.6 40.7 %all-to-all-start.2 = ((bf16[16,40,2048]{2,1,0:T(8,128)(2,1)}), bf16[16,40,2048]{2,1,0:T(8,128)(2,1)S(1)}, u32[]{:S(2)}, u32[]{:S(2)}) async-start(bf16[16,40,2048]{2,1,0:T(8,128)(2,1)} %bitcast.67), calls=%async_computation.2 | async-start | bytes 5242880 | tf_op jit(solution)/shard_map/all_to_all | solution.py:85
  262.3 8.9 %copy-start.6 = (bf16[16,2,1]{0,1,2:T(2,128)(2,1)S(1)}, bf16[16,2,1]{0,1,2:T(2,128)(2,1)}, u32[]{:S(2)}) copy-start(bf16[16,2,1]{0,1,2:T(2,128)(2,1)} %constant.104) | copy-start | bytes 196
  262.3 91.2 %all-to-all-start.5 = ((bf16[16,56,2048]{2,1,0:T(8,128)(2,1)}), bf16[16,56,2048]{2,1,0:T(8,128)(2,1)}, u32[]{:S(2)}, u32[]{:S(2)}) async-start(bf16[16,56,2048]{2,1,0:T(8,128)(2,1)} %bitcast.63), calls=%async_computation.5 | async-start | bytes 7340032 | tf_op jit(solution)/shard_map/all_to_all | solution.py:113
  274.5 81.8 %copy-start.3 = (f32[1,56,2048]{2,1,0:T(8,128)S(1)}, f32[1,56,2048]{2,1,0:T(8,128)}, u32[]{:S(2)}) copy-start(f32[1,56,2048]{2,1,0:T(8,128)} %param.25) | copy-start | bytes 1376260
Sparse Core Ops, SparseCore 0:
  9.8 45.3 all-gather.3
  57.1 73.0 all-gather.5
  132.0 61.6 all-gather.7
